TPU v7x, 32 devices: a whole 2x2x4 slice. The times are simulated.
32 devices in a mesh: ha: 4 (over y, core), wa: 2 (over x), ta: 4 (over z).
Axes of the slice: x: 2, y: 2, z: 4, core: 2. Of those that a mesh axis runs over, the one named last changes fastest.
Arguments:
- video: bfloat16 [16, 96, 64, 256], P('ta', 'ha', 'wa'), may hold values from -210 to 210
- norm_gain: float32 [256], replicated, may hold values from 0.1 to 1.9
- norm_bias: float32 [256], replicated, may hold values from -3 to 3
- spatial_weight: bfloat16 [3, 3, 256, 256], replicated, may hold values from -0.125 to 0.125
- spatial_bias: float32 [256], replicated, may hold values from -3 to 3
- temporal_weight: bfloat16 [3, 256, 256], replicated, may hold values from -0.21875 to 0.21875
- temporal_bias: float32 [256], replicated, may hold values from -3 to 3
Outputs:
- encoded: bfloat16 [16, 96, 64, 256], P('ta', 'ha', 'wa')
All inputs are finite; a program needn't handle non-finite values.
Results may differ from a plain program's by a relative error of at most 0.0054.
Values may be sent and summed in bfloat16 or wider, within the bound.
No kernel may reach another device: no remote copies, remote signals or barrier semaphores. Data moves between devices by JAX's collectives and lax.ppermute only.
A program may use at most 64 MiB of HBM per device.

v0:
```python
import jax
import jax.numpy as jnp
from jax import lax
from jax.sharding import PartitionSpec as P

G = 32


def with_halo(cells, sides, width):
    for axis, dim in sides:
        count = lax.axis_size(axis)
        ends = count - 1
        head = lax.slice_in_dim(cells, 0, width, axis=dim)
        tail = lax.slice_in_dim(cells, cells.shape[dim] - width, cells.shape[dim], axis=dim)
        cells = jnp.concatenate(
            [
                lax.ppermute(tail, axis, [(i, (i + 1) % count) for i in range(ends)]),
                cells,
                lax.ppermute(head, axis, [((i + 1) % count, i) for i in range(ends)]),
            ],
            axis=dim,
        )
    return cells


def shifted(value, axis, steps):
    count = lax.axis_size(axis)
    leading, last = (max(0, -steps), min(count, count - steps))
    return lax.ppermute(value, axis, [(source, source + steps) for source in range(leading, last)])


def convolve(block, spatial_weight, spatial_bias, rows, cols):
    total = jnp.zeros((block.shape[0], rows, cols, spatial_weight.shape[3]), jnp.float32)
    for dy in range(3):
        for dx in range(3):
            total = total + jnp.einsum(
                "fhwc,cd->fhwd",
                block[:, dy : dy + rows, dx : dx + cols],
                spatial_weight[dy, dx],
                preferred_element_type=jnp.float32,
            )
    return (total + spatial_bias).astype(jnp.bfloat16)


def local(
    video, norm_gain, norm_bias, spatial_weight, spatial_bias, temporal_weight, temporal_bias
):
    frames, rows, cols, chans = video.shape
    width = chans // G
    x_values = video.astype(jnp.float32).reshape(frames, rows, cols, G, width)
    count = float(rows * cols * width * lax.axis_size("ha") * lax.axis_size("wa"))
    totals = lax.psum(jnp.sum(x_values, axis=(1, 2, 4)), ("ha", "wa"))
    mean = totals / count
    centered = x_values - mean[:, None, None, :, None]
    spread = lax.psum(jnp.sum(centered * centered, axis=(1, 2, 4)), ("ha", "wa"))
    var = spread / count
    scaled = centered * lax.rsqrt(var + 1e-06)[:, None, None, :, None]
    scaled = scaled.reshape(frames, rows, cols, chans) * norm_gain + norm_bias
    act = jax.nn.silu(scaled).astype(jnp.bfloat16)
    padded = with_halo(act, (("ha", 1), ("wa", 2)), 1)
    spatial = convolve(padded, spatial_weight, spatial_bias, rows, cols)
    earlier = shifted(spatial[frames - 2 :], "ta", 1)
    leading = jnp.concatenate([spatial[:1], spatial[:1]], axis=0)
    earlier = jnp.where(lax.axis_index("ta") == 0, leading, earlier)
    extended = jnp.concatenate([earlier, spatial], axis=0)
    total = jnp.zeros((frames, rows, cols, temporal_weight.shape[2]), jnp.float32)
    for tap in range(3):
        total = total + jnp.einsum(
            "fhwc,cd->fhwd",
            extended[2 - tap : 2 - tap + frames],
            temporal_weight[tap],
            preferred_element_type=jnp.float32,
        )
    return (total + temporal_bias).astype(jnp.bfloat16)


def solution(mesh):
    placed = (P("ta", "ha", "wa", None), P(), P(), P(), P(), P(), P())
    return jax.shard_map(
        local, mesh=mesh, in_specs=placed, out_specs=P("ta", "ha", "wa", None), check_vma=False
    )
```

profile of v0, /device:TPU:27, one launch (start us, length us, event | category | flops | bytes accessed | tf_op | source)
XLA Modules:
  0.0 83.8 jit_solution(10046666974749645342)
XLA Ops:
  0.0 1.8 %convert_reduce_fusion = f32[4,256]{1,0:T(4,128)S(1)} fusion(bf16[4,24,32,256]{3,2,1,0:T(8,128)(2,1)} %param.7), kind=kLoop, calls=%fused_computation.1 | loop fusion | flops 1571840 | bytes 1576960 | tf_op jit(solution)/shard_map/reduce_sum | solution.py:52
  2.0 12.1 %psum.14 = f32[4,32]{1,0:T(4,128)S(1)} all-reduce(f32[4,32]{1,0:T(4,128)S(1)} %reduce_sum.25), channel_id=1, replica_groups=mesh['ha'=4,'wa'=2,'ta'=4] {'ha','wa'}, use_global_device_ids=true, to_apply=%region_2.0 | all-reduce | flops 128 | bytes 1024 | tf_op jit(solution)/shard_map/psum | solution.py:52
  14.9 13.7 %psum.15 = f32[4,32]{1,0:T(4,128)S(1)} all-reduce(f32[4,32]{1,0:T(4,128)S(1)} %reduce_sum.37), channel_id=1, replica_groups=mesh['ha'=4,'wa'=2,'ta'=4] {'ha','wa'}, use_global_device_ids=true, to_apply=%region_5.6 | all-reduce | flops 128 | bytes 1024 | tf_op jit(solution)/shard_map/psum | solution.py:55
  28.8 1.1 %fusion.10 = bf16[4,24,32,256]{3,2,1,0:T(8,128)(2,1)S(1)} fusion(bf16[4,24,32,256]{3,2,1,0:T(8,128)(2,1)S(1)} %copy-done, f32[256]{0:T(256)S(1)} %copy-done.3, f32[256]{0:T(256)S(1)} %copy-done.4, f32[4,256]{1,0:T(4,128)S(1)} %mul.31, f32[4,256]{1,0:T(4,128)S(1)} %sub.15), kind=kLoop, calls=%fused_computation.12 | loop fusion | flops 7864320 | bytes 3155968 | tf_op jit(solution)/shard_map/convert_element_type | solution.py:59
  29.9 4.1 %collective-permute-start = (bf16[4,1,32,256]{3,2,1,0:T(8,128)(2,1)S(1)}, bf16[4,1,32,256]{3,2,1,0:T(8,128)(2,1)S(1)}, u32[]{:S(2)}, u32[]{:S(2)}) collective-permute-start(bf16[4,1,32,256]{3,2,1,0:T(8,128)(2,1)S(1)} %get-tuple-element.9), channel_id=1, source_target_pairs={{0,8},{8,16},{16,24},{1,9},{9,17},{17,25},{2,10},{10,18},{18,26},{... | collective-permute-start | bytes 196616 | tf_op jit(solution)/shard_map/ppermute | solution.py:17
  34.0 1.9 %collective-permute-start.1 = (bf16[4,1,32,256]{3,2,1,0:T(8,128)(2,1)S(1)}, bf16[4,1,32,256]{3,2,1,0:T(8,128)(2,1)S(1)}, u32[]{:S(2)}, u32[]{:S(2)}) collective-permute-start(bf16[4,1,32,256]{3,2,1,0:T(8,128)(2,1)S(1)} %get-tuple-element.10), channel_id=1, source_target_pairs={{8,0},{16,8},{24,16},{9,1},{17,9},{25,17},{10,2},{18,10},{26,18},{... | collective-permute-start | bytes 196616 | tf_op jit(solution)/shard_map/ppermute | solution.py:19
  35.9 0.6 fusion.42
  36.5 3.1 %collective-permute-done.1 = bf16[4,1,32,256]{3,2,1,0:T(8,128)(2,1)S(1)} collective-permute-done((bf16[4,1,32,256]{3,2,1,0:T(8,128)(2,1)S(1)}, bf16[4,1,32,256]{3,2,1,0:T(8,128)(2,1)S(1)}, u32[]{:S(2)}, u32[]{:S(2)}) %collective-permute-start.1) | collective-permute-done | bytes 65568 | tf_op jit(solution)/shard_map/ppermute | solution.py:19
  39.8 1.3 %collective-permute-start.2 = (bf16[4,26,1,256]{3,2,1,0:T(2,128)(2,1)S(1)}, bf16[4,26,1,256]{3,2,1,0:T(2,128)(2,1)S(1)}, u32[]{:S(2)}, u32[]{:S(2)}) collective-permute-start(bf16[4,26,1,256]{3,2,1,0:T(2,128)(2,1)S(1)} %get-tuple-element.8), channel_id=1, source_target_pairs={{0,4},{1,5},{2,6},{3,7},{8,12},{9,13},{10,14},{11,15},{16,20},{17,... | collective-permute-start | bytes 159752 | tf_op jit(solution)/shard_map/ppermute | solution.py:17
  41.1 4.0 %collective-permute-start.3 = (bf16[4,26,1,256]{3,2,1,0:T(2,128)(2,1)S(1)}, bf16[4,26,1,256]{3,2,1,0:T(2,128)(2,1)S(1)}, u32[]{:S(2)}, u32[]{:S(2)}) collective-permute-start(bf16[4,26,1,256]{3,2,1,0:T(2,128)(2,1)S(1)} %get-tuple-element.7), channel_id=1, source_target_pairs={{4,0},{5,1},{6,2},{7,3},{12,8},{13,9},{14,10},{15,11},{20,16},{21,... | collective-permute-start | bytes 159752 | tf_op jit(solution)/shard_map/ppermute | solution.py:19
  45.1 2.3 %fusion.11 = f32[4,24,32,256]{3,2,1,0:T(8,128)} fusion(bf16[4,24,32,256]{3,2,1,0:T(8,128)(2,1)S(1)} %fusion.10, bf16[4,1,32,256]{3,2,1,0:T(8,128)(2,1)S(1)} %collective-permute-done, bf16[3,3,256,256]{3,2,1,0:T(8,128)(2,1)S(1)} %copy-done.1), kind=kOutput, calls=%fused_computation.18 | convolution fusion | flops 405929984 | bytes 4915200 | tf_op jit(solution)/shard_map/fhwc,cd->fhwd/dot_general | solution.py:36
  47.3 2.2 %fusion.15 = f32[4,24,32,256]{3,2,1,0:T(8,128)} fusion(bf16[4,1,32,256]{3,2,1,0:T(8,128)(2,1)S(1)} %collective-permute-done.1, bf16[4,24,32,256]{3,2,1,0:T(8,128)(2,1)S(1)} %fusion.10, bf16[3,3,256,256]{3,2,1,0:T(8,128)(2,1)S(1)} %copy-done.1), kind=kOutput, calls=%fused_computation.22 | convolution fusion | flops 405929984 | bytes 4915200 | tf_op jit(solution)/shard_map/fhwc,cd->fhwd/dot_general | solution.py:36
  49.6 1.3 %pad_maximum_fusion.1 = (bf16[4,26,33,256]{3,2,1,0:T(8,128)(2,1)S(1)}, bf16[4,26,33,256]{3,2,1,0:T(8,128)(2,1)S(1)}) fusion(bf16[4,26,1,256]{3,2,1,0:T(2,128)(2,1)S(1)} %collective-permute-done.3, bf16[4,1,32,256]{3,2,1,0:T(8,128)(2,1)S(1)} %collective-permute-done.1, bf16[4,24,32,256]{3,2,1,0:T(8,128)(2,1)S(1)} %fusion.10, ...), kind=kLoop, calls=%fused_computation.17 | loop fusion | flops 14057472 | bytes 5324800 | tf_op jit(solution)/shard_map/concatenate | solution.py:15
  50.9 0.6 fusion.23
  51.4 0.6 fusion.27
  52.0 0.6 fusion.25
  52.6 0.6 fusion.29
  53.2 2.3 %fusion.31 = f32[4,24,32,256]{3,2,1,0:T(8,128)} fusion(bf16[4,26,33,256]{3,2,1,0:T(8,128)(2,1)S(1)} %get-tuple-element.6, bf16[3,3,256,256]{3,2,1,0:T(8,128)(2,1)S(1)} %copy-done.1), kind=kOutput, calls=%fused_computation.36 | convolution fusion | flops 402653184 | bytes 4849664 | tf_op jit(solution)/shard_map/fhwc,cd->fhwd/dot_general | solution.py:36
  55.5 5.7 %add_convert_fusion.1 = bf16[4,24,32,256]{3,2,1,0:T(8,128)(2,1)S(1)} fusion(f32[4,24,32,256]{3,2,1,0:T(8,128)} %fusion.15, f32[4,24,32,256]{3,2,1,0:T(8,128)S(1)} %fusion.23, f32[4,24,32,256]{3,2,1,0:T(8,128)S(1)} %fusion.25, f32[4,24,32,256]{3,2,1,0:T(8,128)S(1)} %fusion.42, f32[4,24,32,256]{3,2,1,0:T(8,128)S(1)} %fusion.27, ...), kind=kOutput, calls=%fused_computation.14 | convolution fusion | flops 410517504 | bytes 28443648 | tf_op jit(solution)/shard_map/fhwc,cd->fhwd/dot_general | solution.py:36
  61.3 1.4 %collective-permute-start.4 = (bf16[2,24,32,256]{3,2,1,0:T(8,128)(2,1)S(1)}, bf16[2,24,32,256]{3,2,1,0:T(8,128)(2,1)S(1)}, u32[]{:S(2)}, u32[]{:S(2)}) collective-permute-start(bf16[2,24,32,256]{3,2,1,0:T(8,128)(2,1)S(1)} %slice.130), channel_id=1, source_target_pairs={{0,1},{1,2},{2,3},{4,5},{5,6},{6,7},{8,9},{9,10},{10,11},{12,13},{... | collective-permute-start | bytes 2359304 | tf_op jit(solution)/shard_map/ppermute | solution.py:29
  62.8 0.6 fusion.36
  63.4 17.8 %collective-permute-done.4 = bf16[2,24,32,256]{3,2,1,0:T(8,128)(2,1)S(1)} collective-permute-done((bf16[2,24,32,256]{3,2,1,0:T(8,128)(2,1)S(1)}, bf16[2,24,32,256]{3,2,1,0:T(8,128)(2,1)S(1)}, u32[]{:S(2)}, u32[]{:S(2)}) %collective-permute-start.4) | collective-permute-done | bytes 786464 | tf_op jit(solution)/shard_map/ppermute | solution.py:29
  81.3 0.6 fusion.33
  82.0 1.8 %add_convert_fusion = bf16[4,24,32,256]{3,2,1,0:T(8,128)(2,1)} fusion(f32[4,24,32,256]{3,2,1,0:T(8,128)S(1)} %fusion.36, f32[4,24,32,256]{3,2,1,0:T(8,128)S(1)} %fusion.33, f32[256]{0:T(256)S(1)} %copy-done.6, bf16[4,24,32,256]{3,2,1,0:T(8,128)(2,1)S(1)} %add_convert_fusion.1, bf16[2,24,32,256]{3,2,1,0:T(8,128)(2,1)S(1)} %maximum_select_fusion, ...), kind=kOutput, calls=%fused_computation.13 | convolution fusion | flops 410517504 | bytes 10355712 | tf_op jit(solution)/shard_map/fhwc,cd->fhwd/dot_general | solution.py:68
  (33 shorter events, 1.7 us)
Async XLA Ops:
  0.0 14.3 %copy-start = (bf16[4,24,32,256]{3,2,1,0:T(8,128)(2,1)S(1)}, bf16[4,24,32,256]{3,2,1,0:T(8,128)(2,1)}, u32[]{:S(2)}) copy-start(bf16[4,24,32,256]{3,2,1,0:T(8,128)(2,1)} %param.7) | copy-start | bytes 4718596
  0.0 28.8 %copy-start.4 = (f32[256]{0:T(256)S(1)}, f32[256]{0:T(256)}, u32[]{:S(2)}) copy-start(f32[256]{0:T(256)} %param.8) | copy-start | bytes 3076
  0.0 28.8 %copy-start.3 = (f32[256]{0:T(256)S(1)}, f32[256]{0:T(256)}, u32[]{:S(2)}) copy-start(f32[256]{0:T(256)} %param.9) | copy-start | bytes 3076
  14.3 21.6 %copy-start.1 = (bf16[3,3,256,256]{3,2,1,0:T(8,128)(2,1)S(1)}, bf16[3,3,256,256]{3,2,1,0:T(8,128)(2,1)}, u32[]{:S(2)}) copy-start(bf16[3,3,256,256]{3,2,1,0:T(8,128)(2,1)} %param.10) | copy-start | bytes 3538948
  29.9 6.6 %collective-permute-start = (bf16[4,1,32,256]{3,2,1,0:T(8,128)(2,1)S(1)}, bf16[4,1,32,256]{3,2,1,0:T(8,128)(2,1)S(1)}, u32[]{:S(2)}, u32[]{:S(2)}) collective-permute-start(bf16[4,1,32,256]{3,2,1,0:T(8,128)(2,1)S(1)} %get-tuple-element.9), channel_id=1, source_target_pairs={{0,8},{8,16},{16,24},{1,9},{9,17},{17,25},{2,10},{10,18},{18,26},{... | collective-permute-start | bytes 196616 | tf_op jit(solution)/shard_map/ppermute | solution.py:17
  34.0 5.6 %collective-permute-start.1 = (bf16[4,1,32,256]{3,2,1,0:T(8,128)(2,1)S(1)}, bf16[4,1,32,256]{3,2,1,0:T(8,128)(2,1)S(1)}, u32[]{:S(2)}, u32[]{:S(2)}) collective-permute-start(bf16[4,1,32,256]{3,2,1,0:T(8,128)(2,1)S(1)} %get-tuple-element.10), channel_id=1, source_target_pairs={{8,0},{16,8},{24,16},{9,1},{17,9},{25,17},{10,2},{18,10},{26,18},{... | collective-permute-start | bytes 196616 | tf_op jit(solution)/shard_map/ppermute | solution.py:19
  39.8 9.8 %collective-permute-start.2 = (bf16[4,26,1,256]{3,2,1,0:T(2,128)(2,1)S(1)}, bf16[4,26,1,256]{3,2,1,0:T(2,128)(2,1)S(1)}, u32[]{:S(2)}, u32[]{:S(2)}) collective-permute-start(bf16[4,26,1,256]{3,2,1,0:T(2,128)(2,1)S(1)} %get-tuple-element.8), channel_id=1, source_target_pairs={{0,4},{1,5},{2,6},{3,7},{8,12},{9,13},{10,14},{11,15},{16,20},{17,... | collective-permute-start | bytes 159752 | tf_op jit(solution)/shard_map/ppermute | solution.py:17
  41.1 8.5 %collective-permute-start.3 = (bf16[4,26,1,256]{3,2,1,0:T(2,128)(2,1)S(1)}, bf16[4,26,1,256]{3,2,1,0:T(2,128)(2,1)S(1)}, u32[]{:S(2)}, u32[]{:S(2)}) collective-permute-start(bf16[4,26,1,256]{3,2,1,0:T(2,128)(2,1)S(1)} %get-tuple-element.7), channel_id=1, source_target_pairs={{4,0},{5,1},{6,2},{7,3},{12,8},{13,9},{14,10},{15,11},{20,16},{21,... | collective-permute-start | bytes 159752 | tf_op jit(solution)/shard_map/ppermute | solution.py:19
  53.2 2.3 %copy-start.5 = (f32[256]{0:T(256)S(1)}, f32[256]{0:T(256)}, u32[]{:S(2)}) copy-start(f32[256]{0:T(256)} %param.11) | copy-start | bytes 3076
  61.2 1.5 %copy-start.2 = (bf16[3,256,256]{2,1,0:T(8,128)(2,1)S(1)}, bf16[3,256,256]{2,1,0:T(8,128)(2,1)}, u32[]{:S(2)}) copy-start(bf16[3,256,256]{2,1,0:T(8,128)(2,1)} %param.12) | copy-start | bytes 1179652
  61.3 19.9 %collective-permute-start.4 = (bf16[2,24,32,256]{3,2,1,0:T(8,128)(2,1)S(1)}, bf16[2,24,32,256]{3,2,1,0:T(8,128)(2,1)S(1)}, u32[]{:S(2)}, u32[]{:S(2)}) collective-permute-start(bf16[2,24,32,256]{3,2,1,0:T(8,128)(2,1)S(1)} %slice.130), channel_id=1, source_target_pairs={{0,1},{1,2},{2,3},{4,5},{5,6},{6,7},{8,9},{9,10},{10,11},{12,13},{... | collective-permute-start | bytes 2359304 | tf_op jit(solution)/shard_map/ppermute | solution.py:29
  81.3 0.7 copy-start.6
where the time goes:
time: 84 us; the launch traced here: 83.8 us
  blocking collectives  25.8 us (31%)
  waiting for transfers between devices  20.9 us (25%)
  matrix products  18.3 us (22%)
  starting transfers between devices  12.7 us (15%)
  other arithmetic  5.08 us (6%)
    ppermute x1, waiting for transfers between devices, shifted(): lax.ppermute(value, axis, [(source, source + steps) for source in range(l...  17.8 us
    dot_general x9, matrix products, convolve(): jnp.einsum('fhwc,cd->fhwd', block[:, dy:dy + rows, dx:dx + cols], spatial...  15.4 us
    psum x1, blocking collectives, local(): lax.psum(jnp.sum(centered * centered, axis=(1, 2, 4)), ('ha', 'wa'))  13.7 us
    psum x1, blocking collectives, local(): totals = lax.psum(jnp.sum(x_values, axis=(1, 2, 4)), ('ha', 'wa'))  12.1 us
    ppermute x2, starting transfers between devices, with_halo(): lax.ppermute(head, axis, [((i + 1) % count, i) for i in range(ends)])  5.91 us
    ppermute x2, starting transfers between devices, with_halo(): lax.ppermute(tail, axis, [(i, (i + 1) % count) for i in range(ends)])  5.35 us
    ppermute x2, waiting for transfers between devices, with_halo(): lax.ppermute(head, axis, [((i + 1) % count, i) for i in range(ends)])  3.07 us
    dot_general x3, matrix products, local(): jnp.einsum('fhwc,cd->fhwd', extended[2 - tap:2 - tap + frames], temporal_...  2.91 us
  transfers between devices with their start and end apart: 5, of which 2 were waited for; matrix products, arithmetic and copies ran while one was open for 7% of the time, Pallas kernels for 0%

commit v1 on v0

--- a/solution.py
+++ b/solution.py
@@ -49,7 +49,7 @@
     width = chans // G
     x_values = video.astype(jnp.float32).reshape(frames, rows, cols, G, width)
     count = float(rows * cols * width * lax.axis_size("ha") * lax.axis_size("wa"))
-    totals = lax.psum(jnp.sum(x_values, axis=(1, 2, 4)), ("ha", "wa"))
+    totals = lax.psum(lax.psum(jnp.sum(x_values, axis=(1, 2, 4)), "wa"), "ha")
     mean = totals / count
     centered = x_values - mean[:, None, None, :, None]
     spread = lax.psum(jnp.sum(centered * centered, axis=(1, 2, 4)), ("ha", "wa"))

time: 84 us -> 81.4 us (0.969)
  blocking collectives: 25.8 us -> 22.8 us
    psum x1, blocking collectives: 13.7 us -> 12.2 us  [local(): lax.psum(jnp.sum(centered * centered, axis=(1, 2, 4)), ('ha', 'wa'))]
    psum x1 -> x2, blocking collectives: 12.1 us -> 10.6 us  [local(): totals = lax.psum(lax.psum(jnp.sum(x_values, axis=(1, 2, 4)), 'wa'), 'ha')]
where the time goes in v1:
time: 81.4 us; the launch traced here: 81.1 us
  blocking collectives  22.8 us (28%)
  waiting for transfers between devices  20.9 us (26%)
  matrix products  18.4 us (23%)
  starting transfers between devices  13 us (16%)
  other arithmetic  5.08 us (6%)
    ppermute x1, waiting for transfers between devices, shifted(): lax.ppermute(value, axis, [(source, source + steps) for source in range(l...  17.8 us
    dot_general x9, matrix products, convolve(): jnp.einsum('fhwc,cd->fhwd', block[:, dy:dy + rows, dx:dx + cols], spatial...  15.4 us
    psum x1, blocking collectives, local(): lax.psum(jnp.sum(centered * centered, axis=(1, 2, 4)), ('ha', 'wa'))  12.2 us
    psum x2, blocking collectives, local(): totals = lax.psum(lax.psum(jnp.sum(x_values, axis=(1, 2, 4)), 'wa'), 'ha')  10.6 us
    ppermute x2, starting transfers between devices, with_halo(): lax.ppermute(head, axis, [((i + 1) % count, i) for i in range(ends)])  5.91 us
    ppermute x2, starting transfers between devices, with_halo(): lax.ppermute(tail, axis, [(i, (i + 1) % count) for i in range(ends)])  5.66 us
    ppermute x2, waiting for transfers between devices, with_halo(): lax.ppermute(head, axis, [((i + 1) % count, i) for i in range(ends)])  3.06 us
    dot_general x3, matrix products, local(): jnp.einsum('fhwc,cd->fhwd', extended[2 - tap:2 - tap + frames], temporal_...  2.91 us
  transfers between devices with their start and end apart: 5, of which 2 were waited for; matrix products, arithmetic and copies ran while one was open for 7% of the time, Pallas kernels for 0%

profile of v1, /device:TPU:27, one launch (start us, length us, event | category | flops | bytes accessed | tf_op | source)
XLA Modules:
  0.0 81.1 jit_solution(15530076072141326433)
XLA Ops:
  0.0 1.8 %convert_reduce_fusion = f32[4,256]{1,0:T(4,128)S(1)} fusion(bf16[4,24,32,256]{3,2,1,0:T(8,128)(2,1)} %param.7), kind=kLoop, calls=%fused_computation.1 | loop fusion | flops 1571840 | bytes 1576960 | tf_op jit(solution)/shard_map/reduce_sum | solution.py:52
  2.0 3.8 %psum.21 = f32[4,32]{1,0:T(4,128)S(1)} all-reduce(f32[4,32]{1,0:T(4,128)S(1)} %reduce_sum.25), channel_id=1, replica_groups=mesh['ha'=4,'wa'=2,'ta'=4] {'wa'}, use_global_device_ids=true, to_apply=%region_2.0 | all-reduce | flops 128 | bytes 1024 | tf_op jit(solution)/shard_map/psum | solution.py:52
  5.8 6.8 %psum.22 = f32[4,32]{1,0:T(4,128)S(1)} all-reduce(f32[4,32]{1,0:T(4,128)S(1)} %psum.21), channel_id=1, replica_groups=mesh['ha'=4,'wa'=2,'ta'=4] {'ha'}, use_global_device_ids=true, to_apply=%region_3.0 | all-reduce | flops 128 | bytes 1024 | tf_op jit(solution)/shard_map/psum | solution.py:52
  13.5 12.2 %psum.23 = f32[4,32]{1,0:T(4,128)S(1)} all-reduce(f32[4,32]{1,0:T(4,128)S(1)} %reduce_sum.37), channel_id=1, replica_groups=mesh['ha'=4,'wa'=2,'ta'=4] {'ha','wa'}, use_global_device_ids=true, to_apply=%region_6.7 | all-reduce | flops 128 | bytes 1024 | tf_op jit(solution)/shard_map/psum | solution.py:55
  25.9 1.1 %fusion.10 = bf16[4,24,32,256]{3,2,1,0:T(8,128)(2,1)S(1)} fusion(bf16[4,24,32,256]{3,2,1,0:T(8,128)(2,1)S(1)} %copy-done, f32[256]{0:T(256)S(1)} %copy-done.3, f32[256]{0:T(256)S(1)} %copy-done.4, f32[4,256]{1,0:T(4,128)S(1)} %mul.31, f32[4,256]{1,0:T(4,128)S(1)} %sub.15), kind=kLoop, calls=%fused_computation.12 | loop fusion | flops 7864320 | bytes 3155968 | tf_op jit(solution)/shard_map/convert_element_type | solution.py:59
  27.0 4.4 %collective-permute-start = (bf16[4,1,32,256]{3,2,1,0:T(8,128)(2,1)S(1)}, bf16[4,1,32,256]{3,2,1,0:T(8,128)(2,1)S(1)}, u32[]{:S(2)}, u32[]{:S(2)}) collective-permute-start(bf16[4,1,32,256]{3,2,1,0:T(8,128)(2,1)S(1)} %get-tuple-element.9), channel_id=1, source_target_pairs={{0,8},{8,16},{16,24},{1,9},{9,17},{17,25},{2,10},{10,18},{18,26},{... | collective-permute-start | bytes 196616 | tf_op jit(solution)/shard_map/ppermute | solution.py:17
  31.3 1.9 %collective-permute-start.1 = (bf16[4,1,32,256]{3,2,1,0:T(8,128)(2,1)S(1)}, bf16[4,1,32,256]{3,2,1,0:T(8,128)(2,1)S(1)}, u32[]{:S(2)}, u32[]{:S(2)}) collective-permute-start(bf16[4,1,32,256]{3,2,1,0:T(8,128)(2,1)S(1)} %get-tuple-element.10), channel_id=1, source_target_pairs={{8,0},{16,8},{24,16},{9,1},{17,9},{25,17},{10,2},{18,10},{26,18},{... | collective-permute-start | bytes 196616 | tf_op jit(solution)/shard_map/ppermute | solution.py:19
  33.3 0.6 fusion.42
  33.9 3.1 %collective-permute-done.1 = bf16[4,1,32,256]{3,2,1,0:T(8,128)(2,1)S(1)} collective-permute-done((bf16[4,1,32,256]{3,2,1,0:T(8,128)(2,1)S(1)}, bf16[4,1,32,256]{3,2,1,0:T(8,128)(2,1)S(1)}, u32[]{:S(2)}, u32[]{:S(2)}) %collective-permute-start.1) | collective-permute-done | bytes 65568 | tf_op jit(solution)/shard_map/ppermute | solution.py:19
  37.1 1.3 %collective-permute-start.2 = (bf16[4,26,1,256]{3,2,1,0:T(2,128)(2,1)S(1)}, bf16[4,26,1,256]{3,2,1,0:T(2,128)(2,1)S(1)}, u32[]{:S(2)}, u32[]{:S(2)}) collective-permute-start(bf16[4,26,1,256]{3,2,1,0:T(2,128)(2,1)S(1)} %get-tuple-element.8), channel_id=1, source_target_pairs={{0,4},{1,5},{2,6},{3,7},{8,12},{9,13},{10,14},{11,15},{16,20},{17,... | collective-permute-start | bytes 159752 | tf_op jit(solution)/shard_map/ppermute | solution.py:17
  38.4 4.0 %collective-permute-start.3 = (bf16[4,26,1,256]{3,2,1,0:T(2,128)(2,1)S(1)}, bf16[4,26,1,256]{3,2,1,0:T(2,128)(2,1)S(1)}, u32[]{:S(2)}, u32[]{:S(2)}) collective-permute-start(bf16[4,26,1,256]{3,2,1,0:T(2,128)(2,1)S(1)} %get-tuple-element.7), channel_id=1, source_target_pairs={{4,0},{5,1},{6,2},{7,3},{12,8},{13,9},{14,10},{15,11},{20,16},{21,... | collective-permute-start | bytes 159752 | tf_op jit(solution)/shard_map/ppermute | solution.py:19
  42.4 2.3 %fusion.11 = f32[4,24,32,256]{3,2,1,0:T(8,128)} fusion(bf16[4,24,32,256]{3,2,1,0:T(8,128)(2,1)S(1)} %fusion.10, bf16[4,1,32,256]{3,2,1,0:T(8,128)(2,1)S(1)} %collective-permute-done, bf16[3,3,256,256]{3,2,1,0:T(8,128)(2,1)S(1)} %copy-done.1), kind=kOutput, calls=%fused_computation.18 | convolution fusion | flops 405929984 | bytes 4915200 | tf_op jit(solution)/shard_map/fhwc,cd->fhwd/dot_general | solution.py:36
  44.7 2.2 %fusion.15 = f32[4,24,32,256]{3,2,1,0:T(8,128)} fusion(bf16[4,1,32,256]{3,2,1,0:T(8,128)(2,1)S(1)} %collective-permute-done.1, bf16[4,24,32,256]{3,2,1,0:T(8,128)(2,1)S(1)} %fusion.10, bf16[3,3,256,256]{3,2,1,0:T(8,128)(2,1)S(1)} %copy-done.1), kind=kOutput, calls=%fused_computation.22 | convolution fusion | flops 405929984 | bytes 4915200 | tf_op jit(solution)/shard_map/fhwc,cd->fhwd/dot_general | solution.py:36
  46.9 1.3 %pad_maximum_fusion.1 = (bf16[4,26,33,256]{3,2,1,0:T(8,128)(2,1)S(1)}, bf16[4,26,33,256]{3,2,1,0:T(8,128)(2,1)S(1)}) fusion(bf16[4,26,1,256]{3,2,1,0:T(2,128)(2,1)S(1)} %collective-permute-done.3, bf16[4,1,32,256]{3,2,1,0:T(8,128)(2,1)S(1)} %collective-permute-done.1, bf16[4,24,32,256]{3,2,1,0:T(8,128)(2,1)S(1)} %fusion.10, ...), kind=kLoop, calls=%fused_computation.17 | loop fusion | flops 14057472 | bytes 5324800 | tf_op jit(solution)/shard_map/concatenate | solution.py:15
  48.8 0.6 fusion.27
  49.4 0.6 fusion.25
  50.0 0.6 fusion.29
  50.6 2.3 %fusion.31 = f32[4,24,32,256]{3,2,1,0:T(8,128)} fusion(bf16[4,26,33,256]{3,2,1,0:T(8,128)(2,1)S(1)} %get-tuple-element.6, bf16[3,3,256,256]{3,2,1,0:T(8,128)(2,1)S(1)} %copy-done.1), kind=kOutput, calls=%fused_computation.36 | convolution fusion | flops 402653184 | bytes 4849664 | tf_op jit(solution)/shard_map/fhwc,cd->fhwd/dot_general | solution.py:36
  52.8 5.7 %add_convert_fusion.1 = bf16[4,24,32,256]{3,2,1,0:T(8,128)(2,1)S(1)} fusion(f32[4,24,32,256]{3,2,1,0:T(8,128)} %fusion.15, f32[4,24,32,256]{3,2,1,0:T(8,128)S(1)} %fusion.23, f32[4,24,32,256]{3,2,1,0:T(8,128)S(1)} %fusion.25, f32[4,24,32,256]{3,2,1,0:T(8,128)S(1)} %fusion.42, f32[4,24,32,256]{3,2,1,0:T(8,128)S(1)} %fusion.27, ...), kind=kOutput, calls=%fused_computation.14 | convolution fusion | flops 410517504 | bytes 28443648 | tf_op jit(solution)/shard_map/fhwc,cd->fhwd/dot_general | solution.py:36
  58.7 1.4 %collective-permute-start.4 = (bf16[2,24,32,256]{3,2,1,0:T(8,128)(2,1)S(1)}, bf16[2,24,32,256]{3,2,1,0:T(8,128)(2,1)S(1)}, u32[]{:S(2)}, u32[]{:S(2)}) collective-permute-start(bf16[2,24,32,256]{3,2,1,0:T(8,128)(2,1)S(1)} %slice.130), channel_id=1, source_target_pairs={{0,1},{1,2},{2,3},{4,5},{5,6},{6,7},{8,9},{9,10},{10,11},{12,13},{... | collective-permute-start | bytes 2359304 | tf_op jit(solution)/shard_map/ppermute | solution.py:29
  60.2 0.6 fusion.36
  60.7 17.8 %collective-permute-done.4 = bf16[2,24,32,256]{3,2,1,0:T(8,128)(2,1)S(1)} collective-permute-done((bf16[2,24,32,256]{3,2,1,0:T(8,128)(2,1)S(1)}, bf16[2,24,32,256]{3,2,1,0:T(8,128)(2,1)S(1)}, u32[]{:S(2)}, u32[]{:S(2)}) %collective-permute-start.4) | collective-permute-done | bytes 786464 | tf_op jit(solution)/shard_map/ppermute | solution.py:29
  78.7 0.6 fusion.33
  79.4 1.8 %add_convert_fusion = bf16[4,24,32,256]{3,2,1,0:T(8,128)(2,1)} fusion(f32[4,24,32,256]{3,2,1,0:T(8,128)S(1)} %fusion.36, f32[4,24,32,256]{3,2,1,0:T(8,128)S(1)} %fusion.33, f32[256]{0:T(256)S(1)} %copy-done.6, bf16[4,24,32,256]{3,2,1,0:T(8,128)(2,1)S(1)} %add_convert_fusion.1, bf16[2,24,32,256]{3,2,1,0:T(8,128)(2,1)S(1)} %maximum_select_fusion, ...), kind=kOutput, calls=%fused_computation.13 | convolution fusion | flops 410517504 | bytes 10355712 | tf_op jit(solution)/shard_map/fhwc,cd->fhwd/dot_general | solution.py:68
  (34 shorter events, 2.2 us)
Async XLA Ops:
  0.0 12.8 %copy-start = (bf16[4,24,32,256]{3,2,1,0:T(8,128)(2,1)S(1)}, bf16[4,24,32,256]{3,2,1,0:T(8,128)(2,1)}, u32[]{:S(2)}) copy-start(bf16[4,24,32,256]{3,2,1,0:T(8,128)(2,1)} %param.7) | copy-start | bytes 4718596
  0.0 25.8 %copy-start.4 = (f32[256]{0:T(256)S(1)}, f32[256]{0:T(256)}, u32[]{:S(2)}) copy-start(f32[256]{0:T(256)} %param.8) | copy-start | bytes 3076
  0.0 25.8 %copy-start.3 = (f32[256]{0:T(256)S(1)}, f32[256]{0:T(256)}, u32[]{:S(2)}) copy-start(f32[256]{0:T(256)} %param.9) | copy-start | bytes 3076
  12.8 20.4 %copy-start.1 = (bf16[3,3,256,256]{3,2,1,0:T(8,128)(2,1)S(1)}, bf16[3,3,256,256]{3,2,1,0:T(8,128)(2,1)}, u32[]{:S(2)}) copy-start(bf16[3,3,256,256]{3,2,1,0:T(8,128)(2,1)} %param.10) | copy-start | bytes 3538948
  27.0 6.9 %collective-permute-start = (bf16[4,1,32,256]{3,2,1,0:T(8,128)(2,1)S(1)}, bf16[4,1,32,256]{3,2,1,0:T(8,128)(2,1)S(1)}, u32[]{:S(2)}, u32[]{:S(2)}) collective-permute-start(bf16[4,1,32,256]{3,2,1,0:T(8,128)(2,1)S(1)} %get-tuple-element.9), channel_id=1, source_target_pairs={{0,8},{8,16},{16,24},{1,9},{9,17},{17,25},{2,10},{10,18},{18,26},{... | collective-permute-start | bytes 196616 | tf_op jit(solution)/shard_map/ppermute | solution.py:17
  31.3 5.6 %collective-permute-start.1 = (bf16[4,1,32,256]{3,2,1,0:T(8,128)(2,1)S(1)}, bf16[4,1,32,256]{3,2,1,0:T(8,128)(2,1)S(1)}, u32[]{:S(2)}, u32[]{:S(2)}) collective-permute-start(bf16[4,1,32,256]{3,2,1,0:T(8,128)(2,1)S(1)} %get-tuple-element.10), channel_id=1, source_target_pairs={{8,0},{16,8},{24,16},{9,1},{17,9},{25,17},{10,2},{18,10},{26,18},{... | collective-permute-start | bytes 196616 | tf_op jit(solution)/shard_map/ppermute | solution.py:19
  37.1 9.8 %collective-permute-start.2 = (bf16[4,26,1,256]{3,2,1,0:T(2,128)(2,1)S(1)}, bf16[4,26,1,256]{3,2,1,0:T(2,128)(2,1)S(1)}, u32[]{:S(2)}, u32[]{:S(2)}) collective-permute-start(bf16[4,26,1,256]{3,2,1,0:T(2,128)(2,1)S(1)} %get-tuple-element.8), channel_id=1, source_target_pairs={{0,4},{1,5},{2,6},{3,7},{8,12},{9,13},{10,14},{11,15},{16,20},{17,... | collective-permute-start | bytes 159752 | tf_op jit(solution)/shard_map/ppermute | solution.py:17
  38.4 8.5 %collective-permute-start.3 = (bf16[4,26,1,256]{3,2,1,0:T(2,128)(2,1)S(1)}, bf16[4,26,1,256]{3,2,1,0:T(2,128)(2,1)S(1)}, u32[]{:S(2)}, u32[]{:S(2)}) collective-permute-start(bf16[4,26,1,256]{3,2,1,0:T(2,128)(2,1)S(1)} %get-tuple-element.7), channel_id=1, source_target_pairs={{4,0},{5,1},{6,2},{7,3},{12,8},{13,9},{14,10},{15,11},{20,16},{21,... | collective-permute-start | bytes 159752 | tf_op jit(solution)/shard_map/ppermute | solution.py:19
  50.6 2.3 %copy-start.5 = (f32[256]{0:T(256)S(1)}, f32[256]{0:T(256)}, u32[]{:S(2)}) copy-start(f32[256]{0:T(256)} %param.11) | copy-start | bytes 3076
  58.6 1.5 %copy-start.2 = (bf16[3,256,256]{2,1,0:T(8,128)(2,1)S(1)}, bf16[3,256,256]{2,1,0:T(8,128)(2,1)}, u32[]{:S(2)}) copy-start(bf16[3,256,256]{2,1,0:T(8,128)(2,1)} %param.12) | copy-start | bytes 1179652
  58.7 19.9 %collective-permute-start.4 = (bf16[2,24,32,256]{3,2,1,0:T(8,128)(2,1)S(1)}, bf16[2,24,32,256]{3,2,1,0:T(8,128)(2,1)S(1)}, u32[]{:S(2)}, u32[]{:S(2)}) collective-permute-start(bf16[2,24,32,256]{3,2,1,0:T(8,128)(2,1)S(1)} %slice.130), channel_id=1, source_target_pairs={{0,1},{1,2},{2,3},{4,5},{5,6},{6,7},{8,9},{9,10},{10,11},{12,13},{... | collective-permute-start | bytes 2359304 | tf_op jit(solution)/shard_map/ppermute | solution.py:29
  78.7 0.7 copy-start.6
